TPU v7x, 256 devices: a whole 4x4x8 slice. The times are simulated.
256 devices in a mesh: shot: 16 (over z_hi, y, core), dom: 16 (over x, z_lo).
Axes of the slice: x: 4, y: 4, z: 8 (z_hi: 2, z_lo: 4; z = z_hi * 4 + z_lo), core: 2. Of those that a mesh axis runs over, the one named last changes fastest.
Arguments:
- model_slab: float32 [256, 128, 128], P('dom'), may hold values from 0.0225 to 0.17
- wave_prev: float32 [16, 256, 128, 128], P('shot', 'dom'), may hold values from -6 to 6
- wave_now: float32 [16, 256, 128, 128], P('shot', 'dom'), may hold values from -6 to 6
- adjoint_next: float32 [16, 256, 128, 128], P('shot', 'dom'), may hold values from -6 to 6
- adjoint_now: float32 [16, 256, 128, 128], P('shot', 'dom'), may hold values from -6 to 6
- wavelet: float32 [16, 8], P('shot'), may hold values from -12 to 12
- source_cell: int32 [16], P('shot'), may hold values from 0 to 4194303
- receiver_cells: int32 [16, 256], P('shot'), may hold values from 0 to 4194303
- observed: float32 [16, 8, 256], P('shot'), may hold values from -6 to 6
Outputs:
- direction: float32 [256, 128, 128], P('dom')
- new_model: float32 [256, 128, 128], P('dom')
Inputs may be any that keep to these rules, and one draw needn't show every extreme that they name: `source_cell`: flat cell index x * 128 * 128 + y * 128 + z. `receiver_cells`: flat cell indices x * 128 * 128 + y * 128 + z; a cell may repeat.
All inputs are finite; a program needn't handle non-finite values. Where the computation divides by a largest or mean magnitude, that divisor is 1e-20 or more.
Results may differ from a plain program's by a relative error of at most 0.000025.
Values sent between devices are 32-bit elements; how exact they have to be, the bound alone decides.
No kernel may reach another device: no remote copies, remote signals or barrier semaphores. Data moves between devices by JAX's collectives and lax.ppermute only.
A program may use at most 192 MiB of HBM per device.

v0:
```python
import jax
import jax.numpy as jnp
from jax import lax
from jax.sharding import PartitionSpec as P

STEPS = 8
COEFFS = (8.0 / 5.0, -1.0 / 5.0, 8.0 / 315.0, -1.0 / 560.0)
CENTRE = -205.0 / 72.0
STEP_FRACTION = 0.1
EPSILON = 1e-06


def padded_2(cells, sides, width):
    for axis, dim in sides:
        count = lax.axis_size(axis)
        ends = count - 1
        head = lax.slice_in_dim(cells, 0, width, axis=dim)
        tail = lax.slice_in_dim(cells, cells.shape[dim] - width, cells.shape[dim], axis=dim)
        cells = jnp.concatenate(
            [
                lax.ppermute(tail, axis, [(i, (i + 1) % count) for i in range(ends)]),
                cells,
                lax.ppermute(head, axis, [((i + 1) % count, i) for i in range(ends)]),
            ],
            axis=dim,
        )
    return cells


def shifted(field, axis, offset):
    length = field.shape[axis]
    filler_shape = list(field.shape)
    filler_shape[axis] = abs(offset)
    filler = jnp.zeros(filler_shape, field.dtype)
    if offset > 0:
        return jnp.concatenate([lax.slice_in_dim(field, offset, length, axis=axis), filler], axis)
    return jnp.concatenate([filler, lax.slice_in_dim(field, 0, length + offset, axis=axis)], axis)


def laplace(padded):
    rows = padded.shape[0] - 8
    field = padded[4 : 4 + rows]
    total = 3.0 * CENTRE * field
    for index, weight in enumerate(COEFFS):
        offset = index + 1
        total = total + weight * (
            padded[4 + offset : 4 + offset + rows] + padded[4 - offset : 4 - offset + rows]
        )
    for axis in (1, 2):
        for index, weight in enumerate(COEFFS):
            offset = index + 1
            total = total + weight * (shifted(field, axis, offset) + shifted(field, axis, -offset))
    return total


def add_at(field, start_row, targets, amounts):
    count = field.size
    plane = field.shape[1] * field.shape[2]
    relative = targets - start_row * plane
    inside = (relative >= 0) & (relative < count)
    slots = jnp.clip(relative, 0, count - 1)
    values = jnp.where(inside, amounts, 0.0)
    return field.reshape(-1).at[slots].add(values).reshape(field.shape)


def on_device(
    model_slab,
    wave_prev,
    wave_now,
    adjoint_next,
    adjoint_now,
    wavelet,
    source_cell,
    receiver_cells,
    observed,
):
    shape = model_slab.shape
    rows = shape[0]
    cells = shape[0] * shape[1] * shape[2]
    own_row = lax.axis_index("dom") * rows
    first_cell = own_row * shape[1] * shape[2]
    source_one = source_cell[0]
    receivers = receiver_cells[0]
    receiver_local = receivers - first_cell
    receiver_inside = (receiver_local >= 0) & (receiver_local < cells)
    receiver_slots = jnp.clip(receiver_local, 0, cells - 1)
    images = []
    residuals = []
    gradient = jnp.zeros(shape, jnp.float32)
    older, current = (wave_prev[0], wave_now[0])
    for tick in range(STEPS):
        padded = padded_2(current, (("dom", 0),), 4)
        image = laplace(padded)
        newer = 2.0 * current - older + model_slab * image
        newer = add_at(newer, own_row, source_one, wavelet[0, tick])
        values = newer.reshape(-1)[receiver_slots] - observed[0, tick]
        residuals.append(jnp.where(receiver_inside, values, 0.0))
        images.append(image)
        older, current = (current, newer)
    later, present = (adjoint_next[0], adjoint_now[0])
    for tick in reversed(range(STEPS)):
        padded = padded_2(present, (("dom", 0),), 4)
        earlier = 2.0 * present - later + model_slab * laplace(padded)
        earlier = add_at(earlier, own_row, receivers, residuals[tick])
        gradient = gradient + earlier * images[tick]
        later, present = (present, earlier)
    total = lax.psum(gradient, "shot")
    peak = lax.pmax(jnp.max(jnp.abs(total)), "dom")
    direction = total / (peak + EPSILON)
    new_model = model_slab * (1.0 - STEP_FRACTION * direction)
    return (direction, new_model)


def solution(mesh):
    placed = (
        P("dom", None, None),
        P("shot", "dom", None, None),
        P("shot", "dom", None, None),
        P("shot", "dom", None, None),
        P("shot", "dom", None, None),
        P("shot", None),
        P("shot"),
        P("shot", None),
        P("shot", None, None),
    )
    return jax.shard_map(
        on_device,
        mesh=mesh,
        in_specs=placed,
        out_specs=(P("dom", None, None), P("dom", None, None)),
        check_vma=False,
    )
```

profile of v0, /device:TPU:0, one launch (start us, length us, event | category | flops | bytes accessed | tf_op | source)
XLA Modules:
  0.0 704.6 jit_solution(66041510398555331)
XLA Ops:
  10.5 5.3 collective-permute-start.1
  17.1 4.6 collective-permute-start.3
  54.4 9.5 %fusion.432 = (f32[16,128,128]{2,1,0:T(8,128)S(1)}, f32[16,128,128]{2,1,0:T(8,128)}) fusion(f32[1,16,128,128]{3,2,1,0:T(8,128)} %param.26, f32[16,128,128]{2,1,0:T(8,128)} %param.25, f32[1,16,128,128]{3,2,1,0:T(8,128)S(1)} %copy-done.9, f32[16,128,124]{2,1,0:T(8,128)} %get-tuple-element.385, f32[16,128,124]{2,1,0:T(8,128)} %get-tuple-element.384, ...), kind=kLoop, calls=%fused_computation.673 | loop fusion | flops 12845056 | bytes 23265280 | tf_op jit(solution)/shard_map/add | solution.py:94
  78.0 2.1 collective-permute-start.4
  80.7 7.3 %fusion.388 = f32[16,128,128]{2,1,0:T(8,128)S(1)} fusion(f32[16,128,128]{2,1,0:T(8,128)S(1)} %copy-done.13, f32[16,128,128]{2,1,0:T(8,128)S(1)} %bitcast.275, f32[4,128,128]{2,1,0:T(8,128)} %collective-permute-done.1, f32[4,128,128]{2,1,0:T(8,128)S(1)} %collective-permute-done, f32[1,16,128,128]{3,2,1,0:T(8,128)} %param.28, ...), kind=kLoop, calls=%fused_computation.596 | loop fusion | flops 12845056 | bytes 21168128 | tf_op jit(solution)/shard_map/add | solution.py:103
  89.6 5.6 collective-permute-done.4
  95.3 5.5 multiply_add_fusion.7
  104.7 3.9 collective-permute-start.7
  111.4 2.5 collective-permute-done.7
  113.9 10.0 %collective-permute-done.6 = f32[4,128,128]{2,1,0:T(8,128)S(1)} collective-permute-done((f32[4,128,128]{2,1,0:T(8,128)S(1)}, f32[4,128,128]{2,1,0:T(8,128)S(1)}, u32[]{:S(2)}, u32[]{:S(2)}) %collective-permute-start.6) | collective-permute-done | bytes 262176 | tf_op jit(solution)/shard_map/ppermute | solution.py:23
  123.9 7.4 %multiply_add_fusion.6 = (f32[16,128,128]{2,1,0:T(8,128)S(1)}, f32[16,128,128]{2,1,0:T(8,128)}) fusion(f32[16,128,128]{2,1,0:T(8,128)S(1)} %copy-done.14, f32[16,128,128]{2,1,0:T(8,128)S(1)} %bitcast.225, f32[16,128,128]{2,1,0:T(8,128)} %bitcast.235, f32[16,128,124]{2,1,0:T(8,128)S(1)} %get-tuple-element.349, f32[16,128,124]{2,1,0:T(8,128)S(1)} %get-tuple-element.348, ...), kind=kLoop, calls=%fused_computation.683 | loop fusion | flops 12845056 | bytes 22216704 | tf_op jit(solution)/shard_map/add | solution.py:94
  135.2 3.7 collective-permute-start.9
  142.2 2.1 collective-permute-done.9
  144.2 9.8 %collective-permute-done.8 = f32[4,128,128]{2,1,0:T(8,128)S(1)} collective-permute-done((f32[4,128,128]{2,1,0:T(8,128)S(1)}, f32[4,128,128]{2,1,0:T(8,128)S(1)}, u32[]{:S(2)}, u32[]{:S(2)}) %collective-permute-start.8) | collective-permute-done | bytes 262176 | tf_op jit(solution)/shard_map/ppermute | solution.py:23
  154.0 5.4 multiply_add_fusion.5
  163.3 2.3 collective-permute-start.11
  168.4 2.9 collective-permute-done.11
  171.3 9.9 %collective-permute-done.10 = f32[4,128,128]{2,1,0:T(8,128)S(1)} collective-permute-done((f32[4,128,128]{2,1,0:T(8,128)S(1)}, f32[4,128,128]{2,1,0:T(8,128)S(1)}, u32[]{:S(2)}, u32[]{:S(2)}) %collective-permute-start.10) | collective-permute-done | bytes 262176 | tf_op jit(solution)/shard_map/ppermute | solution.py:23
  181.2 5.5 multiply_add_fusion.4
  188.2 10.4 %gather_fusion.3 = f32[256]{0:T(256)S(1)} fusion(f32[262144]{0:T(1024)} %fusion.437, s32[1024]{0:T(1024)S(1)} %pad_clamp_fusion), kind=kCustom, calls=%fused_computation.3 | custom fusion | bytes 3072 | tf_op jit(solution)/shard_map/gather | solution.py:96
  216.2 2.9 fusion.537
  219.3 5.7 collective-permute-done.12
  225.0 7.6 %multiply_add_fusion.3 = (f32[16,128,128]{2,1,0:T(8,128)S(1)}, f32[16,128,128]{2,1,0:T(8,128)}) fusion(f32[16,128,128]{2,1,0:T(8,128)S(1)} %copy-done.17, f32[16,128,128]{2,1,0:T(8,128)S(1)} %bitcast.203, f32[16,128,128]{2,1,0:T(8,128)} %bitcast.40, f32[16,128,124]{2,1,0:T(8,128)S(1)} %get-tuple-element.295, f32[16,128,124]{2,1,0:T(8,128)S(1)} %get-tuple-element.294, ...), kind=kLoop, calls=%fused_computation.680 | loop fusion | flops 12845056 | bytes 22216704 | tf_op jit(solution)/shard_map/add | solution.py:94
  236.7 2.5 collective-permute-start.15
  243.7 6.0 collective-permute-done.14
  249.7 5.5 multiply_add_fusion.2
  259.0 2.3 collective-permute-start.17
  265.9 6.4 collective-permute-done.16
  272.3 5.6 multiply_add_fusion.1
  279.3 10.4 %gather_fusion = f32[256]{0:T(256)S(1)} fusion(f32[262144]{0:T(1024)} %fusion.440, s32[1024]{0:T(1024)S(1)} %pad_clamp_fusion), kind=kCustom, calls=%fused_computation | custom fusion | bytes 3072 | tf_op jit(solution)/shard_map/gather | solution.py:96
  289.8 2.7 scatter_fusion
  300.3 5.7 collective-permute-done.18
  306.0 3.6 fusion.170
  309.5 2.7 scatter_fusion.1
  314.2 2.3 collective-permute-start.21
  318.3 2.5 collective-permute-done.21
  320.8 6.2 collective-permute-done.20
  326.9 3.6 fusion.144
  330.5 2.7 scatter_fusion.2
  335.1 2.3 collective-permute-start.23
  339.4 2.5 collective-permute-done.23
  341.9 6.4 collective-permute-done.22
  348.3 4.3 fusion.118
  352.7 4.4 scatter_fusion.3
  360.4 2.3 collective-permute-start.25
  364.5 2.8 collective-permute-done.25
  367.3 6.6 collective-permute-done.24
  373.9 5.6 fusion.92
  379.5 4.4 scatter_fusion.4
  387.2 2.3 collective-permute-start.27
  394.2 6.5 collective-permute-done.26
  400.7 5.7 fusion.66
  406.4 4.5 scatter_fusion.5
  414.2 2.3 collective-permute-start.29
  421.2 6.5 collective-permute-done.28
  427.7 5.7 fusion.40
  433.4 4.5 scatter_fusion.6
  441.2 2.3 collective-permute-start.31
  448.2 6.5 collective-permute-done.30
  454.7 5.8 fusion.14
  460.4 4.5 scatter_fusion.7
  465.0 7.7 %multiply_add_fusion = f32[16,128,128]{2,1,0:T(8,128)} fusion(f32[16,128,128]{2,1,0:T(8,128)} %bitcast.277, f32[16,128,128]{2,1,0:T(8,128)} %get-tuple-element.115, f32[16,128,128]{2,1,0:T(8,128)} %bitcast.238, f32[16,128,128]{2,1,0:T(8,128)} %get-tuple-element.113, f32[16,128,128]{2,1,0:T(8,128)} %bitcast.171, f32[16,128,128]{2,1,0:T(8,128)} %get-tuple-element.111, ...), kind=kLoop, calls=%fused_computation.677 | loop fusion | flops 3932160 | bytes 17825792 | tf_op jit(solution)/shard_map/add | solution.py:105
  472.7 177.1 %all-reduce.258.cloned.1.call-done = f32[16,128,128]{2,1,0:T(8,128)} async-done(((f32[16,128,128]{2,1,0:T(8,128)}), f32[16,128,128]{2,1,0:T(8,128)}) %all-reduce.258.cloned.1.call-update) | async-done | bytes 1048592 | tf_op jit(solution)/shard_map/psum | solution.py:107
  651.8 43.5 %pmax.7 = f32[]{:T(128)} all-reduce(f32[]{:T(128)} %abs_reduce_fusion), channel_id=1, replica_groups=mesh['shot'=16,'dom'=16] {'dom'}, use_global_device_ids=true, to_apply=%region_10.11 | all-reduce | flops 1 | bytes 8 | tf_op jit(solution)/shard_map/pmax | solution.py:108
  (295 shorter events, 153.3 us)
Async XLA Ops:
  7.2 14.6 %copy-start.11 = (f32[1,16,128,128]{3,2,1,0:T(8,128)S(1)}, f32[1,16,128,128]{3,2,1,0:T(8,128)}, u32[]{:S(2)}) copy-start(f32[1,16,128,128]{3,2,1,0:T(8,128)} %param.29) | copy-start | bytes 3145732
  7.2 14.5 %copy-start.48 = (s32[1,256]{1,0:T(1,128)S(1)}, s32[1,256]{1,0:T(1,128)}, u32[]{:S(2)}) copy-start(s32[1,256]{1,0:T(1,128)} %param.32) | copy-start | bytes 3076
  7.2 642.6 %all-reduce.258.cloned.1.call-start = ((), (), s32[]{:S(2)}) async-start(), calls=%async_computation | async-start | bytes 2097152 | tf_op jit(solution)/shard_map/psum | solution.py:107
  9.2 71.3 %collective-permute-start = (f32[4,128,128]{2,1,0:T(8,128)}, f32[4,128,128]{2,1,0:T(8,128)S(1)}, u32[]{:S(2)}, u32[]{:S(2)}) collective-permute-start(f32[4,128,128]{2,1,0:T(8,128)} %get-tuple-element.402), channel_id=1, source_target_pairs={{1,0},{2,1},{3,2},{4,3},{5,4},{6,5},{7,6},{8,7},{9,8},{10,9},{11,1... | collective-permute-start | bytes 786440 | tf_op jit(solution)/shard_map/ppermute | solution.py:23
  10.5 70.0 %collective-permute-start.1 = (f32[4,128,128]{2,1,0:T(8,128)}, f32[4,128,128]{2,1,0:T(8,128)}, u32[]{:S(2)}, u32[]{:S(2)}) collective-permute-start(f32[4,128,128]{2,1,0:T(8,128)} %get-tuple-element.403), channel_id=1, source_target_pairs={{0,1},{1,2},{2,3},{3,4},{4,5},{5,6},{6,7},{7,8},{8,9},{9,10},{10,1... | collective-permute-start | bytes 786440 | tf_op jit(solution)/shard_map/ppermute | solution.py:21
  15.8 37.8 %collective-permute-start.2 = (f32[4,128,128]{2,1,0:T(8,128)S(1)}, f32[4,128,128]{2,1,0:T(8,128)S(1)}, u32[]{:S(2)}, u32[]{:S(2)}) collective-permute-start(f32[4,128,128]{2,1,0:T(8,128)S(1)} %get-tuple-element.368), channel_id=1, source_target_pairs={{1,0},{2,1},{3,2},{4,3},{5,4},{6,5},{7,6},{8,7},{9,8},{10,9},{11,1... | collective-permute-start | bytes 786440 | tf_op jit(solution)/shard_map/ppermute | solution.py:23
  17.1 36.5 %collective-permute-start.3 = (f32[4,128,128]{2,1,0:T(8,128)S(1)}, f32[4,128,128]{2,1,0:T(8,128)S(1)}, u32[]{:S(2)}, u32[]{:S(2)}) collective-permute-start(f32[4,128,128]{2,1,0:T(8,128)S(1)} %get-tuple-element.369), channel_id=1, source_target_pairs={{0,1},{1,2},{2,3},{3,4},{4,5},{5,6},{6,7},{7,8},{8,9},{9,10},{10,1... | collective-permute-start | bytes 786440 | tf_op jit(solution)/shard_map/ppermute | solution.py:21
  76.1 13.6 %collective-permute-start.5 = (f32[4,128,128]{2,1,0:T(8,128)}, f32[4,128,128]{2,1,0:T(8,128)S(1)}, u32[]{:S(2)}, u32[]{:S(2)}) collective-permute-start(f32[4,128,128]{2,1,0:T(8,128)} %bitcast.18), channel_id=1, source_target_pairs={{0,1},{1,2},{2,3},{3,4},{4,5},{5,6},{6,7},{7,8},{8,9},{9,10},{10,1... | collective-permute-start | bytes 786440 | tf_op jit(solution)/shard_map/ppermute | solution.py:21
  78.0 17.2 %collective-permute-start.4 = (f32[4,128,128]{2,1,0:T(8,128)}, f32[4,128,128]{2,1,0:T(8,128)S(1)}, u32[]{:S(2)}, u32[]{:S(2)}) collective-permute-start(f32[4,128,128]{2,1,0:T(8,128)} %bitcast.17), channel_id=1, source_target_pairs={{1,0},{2,1},{3,2},{4,3},{5,4},{6,5},{7,6},{8,7},{9,8},{10,9},{11,1... | collective-permute-start | bytes 786440 | tf_op jit(solution)/shard_map/ppermute | solution.py:23
  80.6 14.7 %copy-start.32 = (f32[16,125,128]{2,1,0:T(8,128)S(1)}, f32[16,125,128]{2,1,0:T(8,128)}, u32[]{:S(2)}) copy-start(f32[16,125,128]{2,1,0:T(8,128)} %get-tuple-element.357) | copy-start | bytes 3072004
  80.6 14.7 %copy-start.33 = (f32[16,128,126]{2,1,0:T(8,128)S(1)}, f32[16,128,126]{2,1,0:T(8,128)}, u32[]{:S(2)}) copy-start(f32[16,128,126]{2,1,0:T(8,128)} %get-tuple-element.362) | copy-start | bytes 3096580
  80.6 14.7 %copy-start.34 = (f32[16,128,126]{2,1,0:T(8,128)S(1)}, f32[16,128,126]{2,1,0:T(8,128)}, u32[]{:S(2)}) copy-start(f32[16,128,126]{2,1,0:T(8,128)} %get-tuple-element.363) | copy-start | bytes 3096580
  80.6 14.7 %copy-start.35 = (f32[16,126,128]{2,1,0:T(8,128)S(1)}, f32[16,126,128]{2,1,0:T(8,128)}, u32[]{:S(2)}) copy-start(f32[16,126,128]{2,1,0:T(8,128)} %get-tuple-element.354) | copy-start | bytes 3096580
  80.6 14.7 %copy-start.36 = (f32[16,126,128]{2,1,0:T(8,128)S(1)}, f32[16,126,128]{2,1,0:T(8,128)}, u32[]{:S(2)}) copy-start(f32[16,126,128]{2,1,0:T(8,128)} %get-tuple-element.355) | copy-start | bytes 3096580
  80.6 14.7 %copy-start.37 = (f32[16,124,128]{2,1,0:T(8,128)S(1)}, f32[16,124,128]{2,1,0:T(8,128)}, u32[]{:S(2)}) copy-start(f32[16,124,128]{2,1,0:T(8,128)} %get-tuple-element.358) | copy-start | bytes 3047428
  80.6 14.7 %copy-start.38 = (f32[16,124,128]{2,1,0:T(8,128)S(1)}, f32[16,124,128]{2,1,0:T(8,128)}, u32[]{:S(2)}) copy-start(f32[16,124,128]{2,1,0:T(8,128)} %get-tuple-element.359) | copy-start | bytes 3047428
  80.6 14.7 %copy-start.39 = (f32[16,127,128]{2,1,0:T(8,128)S(1)}, f32[16,127,128]{2,1,0:T(8,128)}, u32[]{:S(2)}) copy-start(f32[16,127,128]{2,1,0:T(8,128)} %get-tuple-element.352) | copy-start | bytes 3121156
  80.6 14.7 %copy-start.40 = (f32[16,127,128]{2,1,0:T(8,128)S(1)}, f32[16,127,128]{2,1,0:T(8,128)}, u32[]{:S(2)}) copy-start(f32[16,127,128]{2,1,0:T(8,128)} %get-tuple-element.353) | copy-start | bytes 3121156
  104.7 9.2 %collective-permute-start.7 = (f32[4,128,128]{2,1,0:T(8,128)S(1)}, f32[4,128,128]{2,1,0:T(8,128)S(1)}, u32[]{:S(2)}, u32[]{:S(2)}) collective-permute-start(f32[4,128,128]{2,1,0:T(8,128)S(1)} %bitcast.291), channel_id=1, source_target_pairs={{0,1},{1,2},{2,3},{3,4},{4,5},{5,6},{6,7},{7,8},{8,9},{9,10},{10,1... | collective-permute-start | bytes 786440 | tf_op jit(solution)/shard_map/ppermute | solution.py:21
  108.6 15.3 %copy-start.14 = (f32[16,128,128]{2,1,0:T(8,128)S(1)}, f32[16,128,128]{2,1,0:T(8,128)}, u32[]{:S(2)}) copy-start(f32[16,128,128]{2,1,0:T(8,128)} %param.25) | copy-start | bytes 3145732
  108.6 15.3 %collective-permute-start.6 = (f32[4,128,128]{2,1,0:T(8,128)S(1)}, f32[4,128,128]{2,1,0:T(8,128)S(1)}, u32[]{:S(2)}, u32[]{:S(2)}) collective-permute-start(f32[4,128,128]{2,1,0:T(8,128)S(1)} %bitcast.278), channel_id=1, source_target_pairs={{1,0},{2,1},{3,2},{4,3},{5,4},{6,5},{7,6},{8,7},{9,8},{10,9},{11,1... | collective-permute-start | bytes 786440 | tf_op jit(solution)/shard_map/ppermute | solution.py:23
  135.2 9.0 %collective-permute-start.9 = (f32[4,128,128]{2,1,0:T(8,128)S(1)}, f32[4,128,128]{2,1,0:T(8,128)S(1)}, u32[]{:S(2)}, u32[]{:S(2)}) collective-permute-start(f32[4,128,128]{2,1,0:T(8,128)S(1)} %bitcast.292), channel_id=1, source_target_pairs={{0,1},{1,2},{2,3},{3,4},{4,5},{5,6},{6,7},{7,8},{8,9},{9,10},{10,1... | collective-permute-start | bytes 786440 | tf_op jit(solution)/shard_map/ppermute | solution.py:21
  138.9 15.1 %copy-start.7 = (f32[262144]{0:T(1024)S(1)}, f32[262144]{0:T(1024)}, u32[]{:S(2)}) copy-start(f32[262144]{0:T(1024)} %copy-done.6) | copy-start | bytes 3145732
  138.9 15.1 %copy-start.15 = (f32[16,128,128]{2,1,0:T(8,128)S(1)}, f32[16,128,128]{2,1,0:T(8,128)}, u32[]{:S(2)}) copy-start(f32[16,128,128]{2,1,0:T(8,128)} %param.25) | copy-start | bytes 3145732
  138.9 15.1 %collective-permute-start.8 = (f32[4,128,128]{2,1,0:T(8,128)S(1)}, f32[4,128,128]{2,1,0:T(8,128)S(1)}, u32[]{:S(2)}, u32[]{:S(2)}) collective-permute-start(f32[4,128,128]{2,1,0:T(8,128)S(1)} %bitcast.279), channel_id=1, source_target_pairs={{1,0},{2,1},{3,2},{4,3},{5,4},{6,5},{7,6},{8,7},{9,8},{10,9},{11,1... | collective-permute-start | bytes 786440 | tf_op jit(solution)/shard_map/ppermute | solution.py:23
  163.3 8.0 %collective-permute-start.11 = (f32[4,128,128]{2,1,0:T(8,128)S(1)}, f32[4,128,128]{2,1,0:T(8,128)S(1)}, u32[]{:S(2)}, u32[]{:S(2)}) collective-permute-start(f32[4,128,128]{2,1,0:T(8,128)S(1)} %bitcast.293), channel_id=1, source_target_pairs={{0,1},{1,2},{2,3},{3,4},{4,5},{5,6},{6,7},{7,8},{8,9},{9,10},{10,1... | collective-permute-start | bytes 786440 | tf_op jit(solution)/shard_map/ppermute | solution.py:21
  165.7 15.5 %copy-start.16 = (f32[16,128,128]{2,1,0:T(8,128)S(1)}, f32[16,128,128]{2,1,0:T(8,128)}, u32[]{:S(2)}) copy-start(f32[16,128,128]{2,1,0:T(8,128)} %param.25) | copy-start | bytes 3145732
  165.7 15.5 %collective-permute-start.10 = (f32[4,128,128]{2,1,0:T(8,128)S(1)}, f32[4,128,128]{2,1,0:T(8,128)S(1)}, u32[]{:S(2)}, u32[]{:S(2)}) collective-permute-start(f32[4,128,128]{2,1,0:T(8,128)S(1)} %bitcast.280), channel_id=1, source_target_pairs={{1,0},{2,1},{3,2},{4,3},{5,4},{6,5},{7,6},{8,7},{9,8},{10,9},{11,1... | collective-permute-start | bytes 786440 | tf_op jit(solution)/shard_map/ppermute | solution.py:23
  212.9 6.4 collective-permute-start.13
  214.8 10.2 %copy-start.17 = (f32[16,128,128]{2,1,0:T(8,128)S(1)}, f32[16,128,128]{2,1,0:T(8,128)}, u32[]{:S(2)}) copy-start(f32[16,128,128]{2,1,0:T(8,128)} %param.25) | copy-start | bytes 3145732
  214.8 10.2 %collective-permute-start.12 = (f32[4,128,128]{2,1,0:T(8,128)S(1)}, f32[4,128,128]{2,1,0:T(8,128)S(1)}, u32[]{:S(2)}, u32[]{:S(2)}) collective-permute-start(f32[4,128,128]{2,1,0:T(8,128)S(1)} %bitcast.281), channel_id=1, source_target_pairs={{1,0},{2,1},{3,2},{4,3},{5,4},{6,5},{7,6},{8,7},{9,8},{10,9},{11,1... | collective-permute-start | bytes 786440 | tf_op jit(solution)/shard_map/ppermute | solution.py:23
  236.7 7.0 collective-permute-start.15
  239.2 10.5 %copy-start.18 = (f32[16,128,128]{2,1,0:T(8,128)S(1)}, f32[16,128,128]{2,1,0:T(8,128)}, u32[]{:S(2)}) copy-start(f32[16,128,128]{2,1,0:T(8,128)} %param.25) | copy-start | bytes 3145732
  239.2 10.5 %collective-permute-start.14 = (f32[4,128,128]{2,1,0:T(8,128)S(1)}, f32[4,128,128]{2,1,0:T(8,128)S(1)}, u32[]{:S(2)}, u32[]{:S(2)}) collective-permute-start(f32[4,128,128]{2,1,0:T(8,128)S(1)} %bitcast.282), channel_id=1, source_target_pairs={{1,0},{2,1},{3,2},{4,3},{5,4},{6,5},{7,6},{8,7},{9,8},{10,9},{11,1... | collective-permute-start | bytes 786440 | tf_op jit(solution)/shard_map/ppermute | solution.py:23
  259.0 6.9 collective-permute-start.17
  261.4 11.0 %copy-start.19 = (f32[16,128,128]{2,1,0:T(8,128)S(1)}, f32[16,128,128]{2,1,0:T(8,128)}, u32[]{:S(2)}) copy-start(f32[16,128,128]{2,1,0:T(8,128)} %param.25) | copy-start | bytes 3145732
  261.4 11.0 %collective-permute-start.16 = (f32[4,128,128]{2,1,0:T(8,128)S(1)}, f32[4,128,128]{2,1,0:T(8,128)S(1)}, u32[]{:S(2)}, u32[]{:S(2)}) collective-permute-start(f32[4,128,128]{2,1,0:T(8,128)S(1)} %bitcast.283), channel_id=1, source_target_pairs={{1,0},{2,1},{3,2},{4,3},{5,4},{6,5},{7,6},{8,7},{9,8},{10,9},{11,1... | collective-permute-start | bytes 786440 | tf_op jit(solution)/shard_map/ppermute | solution.py:23
  294.5 5.9 collective-permute-start.19
  296.4 9.6 %copy-start.12 = (f32[1,16,128,128]{3,2,1,0:T(8,128)S(1)}, f32[1,16,128,128]{3,2,1,0:T(8,128)}, u32[]{:S(2)}) copy-start(f32[1,16,128,128]{3,2,1,0:T(8,128)} %param.29) | copy-start | bytes 3145732
  296.4 9.6 %copy-start.20 = (f32[16,128,128]{2,1,0:T(8,128)S(1)}, f32[16,128,128]{2,1,0:T(8,128)}, u32[]{:S(2)}) copy-start(f32[16,128,128]{2,1,0:T(8,128)} %param.25) | copy-start | bytes 3145732
  296.4 9.6 %collective-permute-start.18 = (f32[4,128,128]{2,1,0:T(8,128)S(1)}, f32[4,128,128]{2,1,0:T(8,128)S(1)}, u32[]{:S(2)}, u32[]{:S(2)}) collective-permute-start(f32[4,128,128]{2,1,0:T(8,128)S(1)} %bitcast.284), channel_id=1, source_target_pairs={{1,0},{2,1},{3,2},{4,3},{5,4},{6,5},{7,6},{8,7},{9,8},{10,9},{11,1... | collective-permute-start | bytes 786440 | tf_op jit(solution)/shard_map/ppermute | solution.py:23
  314.2 6.6 collective-permute-start.21
  316.5 10.5 %copy-start.21 = (f32[16,128,128]{2,1,0:T(8,128)S(1)}, f32[16,128,128]{2,1,0:T(8,128)}, u32[]{:S(2)}) copy-start(f32[16,128,128]{2,1,0:T(8,128)} %param.25) | copy-start | bytes 3145732
  316.5 10.4 %collective-permute-start.20 = (f32[4,128,128]{2,1,0:T(8,128)S(1)}, f32[4,128,128]{2,1,0:T(8,128)S(1)}, u32[]{:S(2)}, u32[]{:S(2)}) collective-permute-start(f32[4,128,128]{2,1,0:T(8,128)S(1)} %bitcast.285), channel_id=1, source_target_pairs={{1,0},{2,1},{3,2},{4,3},{5,4},{6,5},{7,6},{8,7},{9,8},{10,9},{11,1... | collective-permute-start | bytes 786440 | tf_op jit(solution)/shard_map/ppermute | solution.py:23
  335.1 6.8 collective-permute-start.23
  337.4 10.9 %copy-start.22 = (f32[16,128,128]{2,1,0:T(8,128)S(1)}, f32[16,128,128]{2,1,0:T(8,128)}, u32[]{:S(2)}) copy-start(f32[16,128,128]{2,1,0:T(8,128)} %param.25) | copy-start | bytes 3145732
  337.4 10.9 %collective-permute-start.22 = (f32[4,128,128]{2,1,0:T(8,128)S(1)}, f32[4,128,128]{2,1,0:T(8,128)S(1)}, u32[]{:S(2)}, u32[]{:S(2)}) collective-permute-start(f32[4,128,128]{2,1,0:T(8,128)S(1)} %bitcast.286), channel_id=1, source_target_pairs={{1,0},{2,1},{3,2},{4,3},{5,4},{6,5},{7,6},{8,7},{9,8},{10,9},{11,1... | collective-permute-start | bytes 786440 | tf_op jit(solution)/shard_map/ppermute | solution.py:23
  360.4 6.9 collective-permute-start.25
  362.7 11.2 %copy-start.23 = (f32[16,128,128]{2,1,0:T(8,128)S(1)}, f32[16,128,128]{2,1,0:T(8,128)}, u32[]{:S(2)}) copy-start(f32[16,128,128]{2,1,0:T(8,128)} %param.25) | copy-start | bytes 3145732
  362.7 11.2 %collective-permute-start.24 = (f32[4,128,128]{2,1,0:T(8,128)S(1)}, f32[4,128,128]{2,1,0:T(8,128)}, u32[]{:S(2)}, u32[]{:S(2)}) collective-permute-start(f32[4,128,128]{2,1,0:T(8,128)S(1)} %bitcast.287), channel_id=1, source_target_pairs={{1,0},{2,1},{3,2},{4,3},{5,4},{6,5},{7,6},{8,7},{9,8},{10,9},{11,1... | collective-permute-start | bytes 786440 | tf_op jit(solution)/shard_map/ppermute | solution.py:23
  387.2 7.0 collective-permute-start.27
  389.5 11.2 %copy-start.1 = (f32[262144]{0:T(1024)S(1)}, f32[262144]{0:T(1024)}, u32[]{:S(2)}) copy-start(f32[262144]{0:T(1024)} %scatter_fusion.3) | copy-start | bytes 3145732
  389.5 11.2 %copy-start.24 = (f32[16,128,128]{2,1,0:T(8,128)S(1)}, f32[16,128,128]{2,1,0:T(8,128)}, u32[]{:S(2)}) copy-start(f32[16,128,128]{2,1,0:T(8,128)} %param.25) | copy-start | bytes 3145732
  389.5 11.2 %collective-permute-start.26 = (f32[4,128,128]{2,1,0:T(8,128)S(1)}, f32[4,128,128]{2,1,0:T(8,128)}, u32[]{:S(2)}, u32[]{:S(2)}) collective-permute-start(f32[4,128,128]{2,1,0:T(8,128)S(1)} %bitcast.288), channel_id=1, source_target_pairs={{1,0},{2,1},{3,2},{4,3},{5,4},{6,5},{7,6},{8,7},{9,8},{10,9},{11,1... | collective-permute-start | bytes 786440 | tf_op jit(solution)/shard_map/ppermute | solution.py:23
  414.2 7.0 collective-permute-start.29
  416.5 11.2 %copy-start.3 = (f32[262144]{0:T(1024)S(1)}, f32[262144]{0:T(1024)}, u32[]{:S(2)}) copy-start(f32[262144]{0:T(1024)} %scatter_fusion.4) | copy-start | bytes 3145732
  416.5 11.2 %copy-start.25 = (f32[16,128,128]{2,1,0:T(8,128)S(1)}, f32[16,128,128]{2,1,0:T(8,128)}, u32[]{:S(2)}) copy-start(f32[16,128,128]{2,1,0:T(8,128)} %param.25) | copy-start | bytes 3145732
  416.5 11.2 %collective-permute-start.28 = (f32[4,128,128]{2,1,0:T(8,128)S(1)}, f32[4,128,128]{2,1,0:T(8,128)}, u32[]{:S(2)}, u32[]{:S(2)}) collective-permute-start(f32[4,128,128]{2,1,0:T(8,128)S(1)} %bitcast.289), channel_id=1, source_target_pairs={{1,0},{2,1},{3,2},{4,3},{5,4},{6,5},{7,6},{8,7},{9,8},{10,9},{11,1... | collective-permute-start | bytes 786440 | tf_op jit(solution)/shard_map/ppermute | solution.py:23
  441.2 7.0 collective-permute-start.31
  443.5 11.2 %copy-start.5 = (f32[262144]{0:T(1024)S(1)}, f32[262144]{0:T(1024)}, u32[]{:S(2)}) copy-start(f32[262144]{0:T(1024)} %scatter_fusion.5) | copy-start | bytes 3145732
  443.5 11.2 %copy-start.26 = (f32[16,128,128]{2,1,0:T(8,128)S(1)}, f32[16,128,128]{2,1,0:T(8,128)}, u32[]{:S(2)}) copy-start(f32[16,128,128]{2,1,0:T(8,128)} %param.25) | copy-start | bytes 3145732
  443.5 11.2 %collective-permute-start.30 = (f32[4,128,128]{2,1,0:T(8,128)S(1)}, f32[4,128,128]{2,1,0:T(8,128)}, u32[]{:S(2)}, u32[]{:S(2)}) collective-permute-start(f32[4,128,128]{2,1,0:T(8,128)S(1)} %bitcast.290), channel_id=1, source_target_pairs={{1,0},{2,1},{3,2},{4,3},{5,4},{6,5},{7,6},{8,7},{9,8},{10,9},{11,1... | collective-permute-start | bytes 786440 | tf_op jit(solution)/shard_map/ppermute | solution.py:23
  472.7 223.3 %copy-start.27 = (f32[16,128,128]{2,1,0:T(8,128)S(1)}, f32[16,128,128]{2,1,0:T(8,128)}, u32[]{:S(2)}) copy-start(f32[16,128,128]{2,1,0:T(8,128)} %param.25) | copy-start | bytes 3145732
  649.8 46.2 %copy-start.28 = (f32[16,128,128]{2,1,0:T(8,128)S(1)}, f32[16,128,128]{2,1,0:T(8,128)}, u32[]{:S(2)}) copy-start(f32[16,128,128]{2,1,0:T(8,128)} %all-reduce.258.cloned.1.call-done) | copy-start | bytes 3145732
  (18 other events, 73.9 us)
Sparse Core Ops, SparseCore 0:
  472.9 176.9 all-reduce.257
where the time goes:
time: 713 us; the launch traced here: 705 us
  waiting for transfers between devices  301 us (42%)
  other arithmetic  139 us (19%)
  local copies, waits for them, and re-layouts  131 us (18%)
  starting transfers between devices  68.4 us (10%)
  blocking collectives  43.5 us (6%)
  between operations  22.2 us (3%)
    psum x1, waiting for transfers between devices, on_device(): total = lax.psum(gradient, 'shot')  177 us
    ppermute x16, waiting for transfers between devices, padded_2(): lax.ppermute(head, axis, [((i + 1) % count, i) for i in range(ends)])  97.7 us
    slice x128, local copies, waits for them, and re-layouts, shifted(): lax.slice_in_dim(field, offset, length, axis=axis)  88.1 us
    add x8, other arithmetic, on_device(): newer = 2.0 * current - older + model_slab * image  51.9 us
    ppermute x16, starting transfers between devices, padded_2(): lax.ppermute(tail, axis, [(i, (i + 1) % count) for i in range(ends)])  44 us
    pmax x1, blocking collectives, on_device(): peak = lax.pmax(jnp.max(jnp.abs(total)), 'dom')  43.5 us
    add x8, other arithmetic, on_device(): earlier = 2.0 * present - later + model_slab * laplace(padded)  41.5 us
    scatter-add x16, other arithmetic, add_at(): return field.reshape(-1).at[slots].add(values).reshape(field.shape)  34.6 us
  transfers between devices with their start and end apart: 33, of which 28 were waited for; matrix products, arithmetic and copies ran while one was open for 10% of the time, Pallas kernels for 0%

commit v1 on v0

--- a/solution.py
+++ b/solution.py
@@ -104,7 +104,7 @@
         earlier = add_at(earlier, own_row, receivers, residuals[tick])
         gradient = gradient + earlier * images[tick]
         later, present = (present, earlier)
-    total = lax.psum(gradient, "shot")
+    total = lax.all_gather(gradient, "shot").sum(axis=0)
     peak = lax.pmax(jnp.max(jnp.abs(total)), "dom")
     direction = total / (peak + EPSILON)
     new_model = model_slab * (1.0 - STEP_FRACTION * direction)

time: 713 us -> 717 us (level)
    psum x1 -> x0, waiting for transfers between devices: 177 us -> none  [on_device(): total = lax.psum(gradient, 'shot')]
    all_gather x0 -> x1, waiting for transfers between devices: none -> 171 us  [on_device(): total = lax.all_gather(gradient, 'shot').sum(axis=0)]
    reduce_sum x0 -> x1, other arithmetic: none -> 7.44 us  [on_device(): total = lax.all_gather(gradient, 'shot').sum(axis=0)]
where the time goes in v1:
time: 717 us; the launch traced here: 707 us
  waiting for transfers between devices  300 us (42%)
  other arithmetic  146 us (20%)
  local copies, waits for them, and re-layouts  133 us (19%)
  starting transfers between devices  67.7 us (9%)
  blocking collectives  38.6 us (5%)
  between operations  22.1 us (3%)
    all_gather x1, waiting for transfers between devices, on_device(): total = lax.all_gather(gradient, 'shot').sum(axis=0)  171 us
    ppermute x16, waiting for transfers between devices, padded_2(): lax.ppermute(head, axis, [((i + 1) % count, i) for i in range(ends)])  96.9 us
    slice x128, local copies, waits for them, and re-layouts, shifted(): lax.slice_in_dim(field, offset, length, axis=axis)  83.1 us
    add x8, other arithmetic, on_device(): newer = 2.0 * current - older + model_slab * image  52.7 us
    ppermute x16, starting transfers between devices, padded_2(): lax.ppermute(tail, axis, [(i, (i + 1) % count) for i in range(ends)])  43.7 us
    add x8, other arithmetic, on_device(): earlier = 2.0 * present - later + model_slab * laplace(padded)  39.4 us
    pmax x1, blocking collectives, on_device(): peak = lax.pmax(jnp.max(jnp.abs(total)), 'dom')  38.6 us
    gather x8, local copies, waits for them, and re-layouts, on_device(): values = newer.reshape(-1)[receiver_slots] - observed[0, tick]  35.3 us
  transfers between devices with their start and end apart: 33, of which 28 were waited for; matrix products, arithmetic and copies ran while one was open for 10% of the time, Pallas kernels for 0%

profile of v1, /device:TPU:0, one launch (start us, length us, event | category | flops | bytes accessed | tf_op | source)
XLA Modules:
  0.0 706.8 jit_solution(5551761561673974648)
XLA Ops:
  10.5 5.3 collective-permute-start.1
  17.2 4.6 collective-permute-start.3
  55.1 9.5 %fusion.432 = (f32[16,128,128]{2,1,0:T(8,128)S(1)}, f32[16,128,128]{2,1,0:T(8,128)}) fusion(f32[1,16,128,128]{3,2,1,0:T(8,128)} %param.26, f32[16,128,128]{2,1,0:T(8,128)} %param.25, f32[1,16,128,128]{3,2,1,0:T(8,128)S(1)} %copy-done.9, f32[16,128,124]{2,1,0:T(8,128)} %get-tuple-element.385, f32[16,128,124]{2,1,0:T(8,128)} %get-tuple-element.384, ...), kind=kLoop, calls=%fused_computation.673 | loop fusion | flops 12845056 | bytes 23265280 | tf_op jit(solution)/shard_map/add | solution.py:94
  75.1 2.3 gather_fusion.7
  77.4 2.6 collective-permute-start.5
  82.3 7.3 %fusion.388 = f32[16,128,128]{2,1,0:T(8,128)S(1)} fusion(f32[16,128,128]{2,1,0:T(8,128)S(1)} %copy-done.13, f32[16,128,128]{2,1,0:T(8,128)S(1)} %bitcast.276, f32[4,128,128]{2,1,0:T(8,128)} %collective-permute-done.1, f32[4,128,128]{2,1,0:T(8,128)S(1)} %collective-permute-done, f32[1,16,128,128]{3,2,1,0:T(8,128)} %param.28, ...), kind=kLoop, calls=%fused_computation.596 | loop fusion | flops 12845056 | bytes 21168128 | tf_op jit(solution)/shard_map/add | solution.py:103
  90.9 5.7 collective-permute-done.4
  96.8 5.5 multiply_add_fusion.7
  102.5 2.3 gather_fusion.6
  106.7 3.9 collective-permute-start.7
  112.5 3.5 collective-permute-done.7
  115.9 9.9 %collective-permute-done.6 = f32[4,128,128]{2,1,0:T(8,128)S(1)} collective-permute-done((f32[4,128,128]{2,1,0:T(8,128)S(1)}, f32[4,128,128]{2,1,0:T(8,128)S(1)}, u32[]{:S(2)}, u32[]{:S(2)}) %collective-permute-start.6) | collective-permute-done | bytes 262176 | tf_op jit(solution)/shard_map/ppermute | solution.py:23
  126.5 7.5 %multiply_add_fusion.6 = (f32[16,128,128]{2,1,0:T(8,128)S(1)}, f32[16,128,128]{2,1,0:T(8,128)}) fusion(f32[16,128,128]{2,1,0:T(8,128)S(1)} %copy-done.14, f32[16,128,128]{2,1,0:T(8,128)S(1)} %bitcast.226, f32[16,128,128]{2,1,0:T(8,128)} %bitcast.236, f32[16,128,124]{2,1,0:T(8,128)S(1)} %get-tuple-element.349, f32[16,128,124]{2,1,0:T(8,128)S(1)} %get-tuple-element.348, ...), kind=kLoop, calls=%fused_computation.683 | loop fusion | flops 12845056 | bytes 22216704 | tf_op jit(solution)/shard_map/add | solution.py:94
  134.3 2.3 gather_fusion.5
  138.6 2.9 collective-permute-start.9
  146.9 9.8 %collective-permute-done.8 = f32[4,128,128]{2,1,0:T(8,128)S(1)} collective-permute-done((f32[4,128,128]{2,1,0:T(8,128)S(1)}, f32[4,128,128]{2,1,0:T(8,128)S(1)}, u32[]{:S(2)}, u32[]{:S(2)}) %collective-permute-start.8) | collective-permute-done | bytes 262176 | tf_op jit(solution)/shard_map/ppermute | solution.py:23
  157.3 5.5 multiply_add_fusion.5
  163.0 2.3 gather_fusion.4
  167.3 3.0 collective-permute-start.11
  172.1 3.2 collective-permute-done.11
  175.2 10.7 %collective-permute-done.10 = f32[4,128,128]{2,1,0:T(8,128)} collective-permute-done((f32[4,128,128]{2,1,0:T(8,128)S(1)}, f32[4,128,128]{2,1,0:T(8,128)}, u32[]{:S(2)}, u32[]{:S(2)}) %collective-permute-start.10) | collective-permute-done | bytes 262176 | tf_op jit(solution)/shard_map/ppermute | solution.py:23
  185.9 5.7 multiply_add_fusion.4
  193.1 10.9 %gather_fusion.3 = f32[256]{0:T(256)} fusion(f32[262144]{0:T(1024)} %fusion.437, s32[1024]{0:T(1024)S(1)} %pad_clamp_fusion), kind=kCustom, calls=%fused_computation.3 | custom fusion | bytes 3072 | tf_op jit(solution)/shard_map/gather | solution.py:96
  225.8 5.1 collective-permute-done.12
  231.7 7.7 %multiply_add_fusion.3 = (f32[16,128,128]{2,1,0:T(8,128)S(1)}, f32[16,128,128]{2,1,0:T(8,128)}) fusion(f32[16,128,128]{2,1,0:T(8,128)S(1)} %copy-done.17, f32[16,128,128]{2,1,0:T(8,128)S(1)} %bitcast.204, f32[16,128,128]{2,1,0:T(8,128)} %bitcast.40, f32[16,128,124]{2,1,0:T(8,128)S(1)} %get-tuple-element.295, f32[16,128,124]{2,1,0:T(8,128)S(1)} %get-tuple-element.294, ...), kind=kLoop, calls=%fused_computation.680 | loop fusion | flops 12845056 | bytes 22216704 | tf_op jit(solution)/shard_map/add | solution.py:94
  240.0 2.3 gather_fusion.2
  248.0 3.1 collective-permute-done.15
  251.0 5.8 collective-permute-done.14
  257.5 5.6 multiply_add_fusion.2
  263.2 2.3 gather_fusion.1
  267.5 3.0 collective-permute-start.17
  274.5 6.7 collective-permute-done.16
  281.2 5.6 multiply_add_fusion.1
  288.3 10.4 %gather_fusion = f32[256]{0:T(256)S(1)} fusion(f32[262144]{0:T(1024)} %fusion.440, s32[1024]{0:T(1024)S(1)} %pad_clamp_fusion), kind=kCustom, calls=%fused_computation | custom fusion | bytes 3072 | tf_op jit(solution)/shard_map/gather | solution.py:96
  299.4 2.7 scatter_fusion
  307.7 2.4 collective-permute-done.19
  310.1 5.4 collective-permute-done.18
  315.5 3.6 fusion.170
  319.1 2.7 scatter_fusion.1
  327.7 2.6 collective-permute-done.21
  330.2 6.0 collective-permute-done.20
  336.2 3.6 fusion.144
  339.8 2.7 scatter_fusion.2
  348.8 2.5 collective-permute-done.23
  351.3 6.2 collective-permute-done.22
  357.5 4.4 fusion.118
  361.9 4.5 scatter_fusion.3
  373.8 2.8 collective-permute-done.25
  376.6 6.3 collective-permute-done.24
  383.0 4.3 fusion.92
  387.2 4.4 scatter_fusion.4
  402.0 6.4 collective-permute-done.26
  408.4 5.5 fusion.66
  413.8 4.5 scatter_fusion.5
  428.6 6.5 collective-permute-done.28
  435.1 5.5 fusion.40
  440.5 4.4 scatter_fusion.6
  455.3 6.4 collective-permute-done.30
  461.7 5.4 fusion.14
  467.2 4.5 scatter_fusion.7
  471.6 7.8 %multiply_add_fusion = f32[16,128,128]{2,1,0:T(8,128)} fusion(f32[16,128,128]{2,1,0:T(8,128)} %bitcast.279, f32[16,128,128]{2,1,0:T(8,128)} %get-tuple-element.115, f32[16,128,128]{2,1,0:T(8,128)} %bitcast.239, f32[16,128,128]{2,1,0:T(8,128)} %get-tuple-element.113, f32[16,128,128]{2,1,0:T(8,128)} %bitcast.172, f32[16,128,128]{2,1,0:T(8,128)} %get-tuple-element.111, ...), kind=kLoop, calls=%fused_computation.677 | loop fusion | flops 3932160 | bytes 17825792 | tf_op jit(solution)/shard_map/add | solution.py:105
  479.5 171.3 %all-gather.3.cloned.1.call-done = f32[256,128,128]{2,1,0:T(8,128)} async-done(((f32[16,128,128]{2,1,0:T(8,128)}), f32[256,128,128]{2,1,0:T(8,128)}) %all-gather.3.cloned.1.call-update) | async-done | bytes 16777232 | tf_op jit(solution)/shard_map/all_gather | solution.py:107
  650.7 7.4 %reduce_sum.9 = f32[16,128,128]{2,1,0:T(8,128)S(1)} reduce(f32[16,16,128,128]{3,2,1,0:T(8,128)} %bitcast.277, f32[]{:T(128)} %constant.180.clone.1), dimensions={0}, to_apply=%region_8.9 | reduce | flops 3932160 | bytes 17825796 | tf_op jit(solution)/shard_map/reduce_sum | solution.py:107
  658.9 38.6 %pmax.7 = f32[]{:T(128)} all-reduce(f32[]{:T(128)} %abs_reduce_fusion), channel_id=1, replica_groups=mesh['shot'=16,'dom'=16] {'dom'}, use_global_device_ids=true, to_apply=%region_10.11 | all-reduce | flops 1 | bytes 8 | tf_op jit(solution)/shard_map/pmax | solution.py:108
  (310 shorter events, 159.7 us)
Async XLA Ops:
  7.2 15.1 %copy-start.11 = (f32[1,16,128,128]{3,2,1,0:T(8,128)S(1)}, f32[1,16,128,128]{3,2,1,0:T(8,128)}, u32[]{:S(2)}) copy-start(f32[1,16,128,128]{3,2,1,0:T(8,128)} %param.29) | copy-start | bytes 3145732
  7.2 14.5 %copy-start.55 = (s32[1,256]{1,0:T(1,128)S(1)}, s32[1,256]{1,0:T(1,128)}, u32[]{:S(2)}) copy-start(s32[1,256]{1,0:T(1,128)} %param.32) | copy-start | bytes 3076
  7.2 643.5 %all-gather.3.cloned.1.call-start = ((), (), s32[]{:S(2)}) async-start(), calls=%async_computation | async-start | bytes 17825792 | tf_op jit(solution)/shard_map/all_gather | solution.py:107
  9.2 72.9 %collective-permute-start = (f32[4,128,128]{2,1,0:T(8,128)}, f32[4,128,128]{2,1,0:T(8,128)S(1)}, u32[]{:S(2)}, u32[]{:S(2)}) collective-permute-start(f32[4,128,128]{2,1,0:T(8,128)} %get-tuple-element.402), channel_id=1, source_target_pairs={{1,0},{2,1},{3,2},{4,3},{5,4},{6,5},{7,6},{8,7},{9,8},{10,9},{11,1... | collective-permute-start | bytes 786440 | tf_op jit(solution)/shard_map/ppermute | solution.py:23
  10.5 71.6 %collective-permute-start.1 = (f32[4,128,128]{2,1,0:T(8,128)}, f32[4,128,128]{2,1,0:T(8,128)}, u32[]{:S(2)}, u32[]{:S(2)}) collective-permute-start(f32[4,128,128]{2,1,0:T(8,128)} %get-tuple-element.403), channel_id=1, source_target_pairs={{0,1},{1,2},{2,3},{3,4},{4,5},{5,6},{6,7},{7,8},{8,9},{9,10},{10,1... | collective-permute-start | bytes 786440 | tf_op jit(solution)/shard_map/ppermute | solution.py:21
  15.9 38.5 %collective-permute-start.2 = (f32[4,128,128]{2,1,0:T(8,128)S(1)}, f32[4,128,128]{2,1,0:T(8,128)S(1)}, u32[]{:S(2)}, u32[]{:S(2)}) collective-permute-start(f32[4,128,128]{2,1,0:T(8,128)S(1)} %get-tuple-element.368), channel_id=1, source_target_pairs={{1,0},{2,1},{3,2},{4,3},{5,4},{6,5},{7,6},{8,7},{9,8},{10,9},{11,1... | collective-permute-start | bytes 786440 | tf_op jit(solution)/shard_map/ppermute | solution.py:23
  17.2 37.2 %collective-permute-start.3 = (f32[4,128,128]{2,1,0:T(8,128)S(1)}, f32[4,128,128]{2,1,0:T(8,128)S(1)}, u32[]{:S(2)}, u32[]{:S(2)}) collective-permute-start(f32[4,128,128]{2,1,0:T(8,128)S(1)} %get-tuple-element.369), channel_id=1, source_target_pairs={{0,1},{1,2},{2,3},{3,4},{4,5},{5,6},{6,7},{7,8},{8,9},{9,10},{10,1... | collective-permute-start | bytes 786440 | tf_op jit(solution)/shard_map/ppermute | solution.py:21
  77.4 13.5 %collective-permute-start.5 = (f32[4,128,128]{2,1,0:T(8,128)}, f32[4,128,128]{2,1,0:T(8,128)}, u32[]{:S(2)}, u32[]{:S(2)}) collective-permute-start(f32[4,128,128]{2,1,0:T(8,128)} %bitcast.18), channel_id=1, source_target_pairs={{0,1},{1,2},{2,3},{3,4},{4,5},{5,6},{6,7},{7,8},{8,9},{9,10},{10,1... | collective-permute-start | bytes 786440 | tf_op jit(solution)/shard_map/ppermute | solution.py:21
  80.0 16.6 %collective-permute-start.4 = (f32[4,128,128]{2,1,0:T(8,128)}, f32[4,128,128]{2,1,0:T(8,128)}, u32[]{:S(2)}, u32[]{:S(2)}) collective-permute-start(f32[4,128,128]{2,1,0:T(8,128)} %bitcast.17), channel_id=1, source_target_pairs={{1,0},{2,1},{3,2},{4,3},{5,4},{6,5},{7,6},{8,7},{9,8},{10,9},{11,1... | collective-permute-start | bytes 786440 | tf_op jit(solution)/shard_map/ppermute | solution.py:23
  82.2 14.5 %copy-start.31 = (f32[16,125,128]{2,1,0:T(8,128)S(1)}, f32[16,125,128]{2,1,0:T(8,128)}, u32[]{:S(2)}) copy-start(f32[16,125,128]{2,1,0:T(8,128)} %get-tuple-element.357) | copy-start | bytes 3072004
  82.2 14.5 %copy-start.32 = (f32[16,128,126]{2,1,0:T(8,128)S(1)}, f32[16,128,126]{2,1,0:T(8,128)}, u32[]{:S(2)}) copy-start(f32[16,128,126]{2,1,0:T(8,128)} %get-tuple-element.362) | copy-start | bytes 3096580
  82.2 14.5 %copy-start.33 = (f32[16,128,126]{2,1,0:T(8,128)S(1)}, f32[16,128,126]{2,1,0:T(8,128)}, u32[]{:S(2)}) copy-start(f32[16,128,126]{2,1,0:T(8,128)} %get-tuple-element.363) | copy-start | bytes 3096580
  82.2 14.5 %copy-start.34 = (f32[16,126,128]{2,1,0:T(8,128)S(1)}, f32[16,126,128]{2,1,0:T(8,128)}, u32[]{:S(2)}) copy-start(f32[16,126,128]{2,1,0:T(8,128)} %get-tuple-element.354) | copy-start | bytes 3096580
  82.2 14.5 %copy-start.35 = (f32[16,126,128]{2,1,0:T(8,128)S(1)}, f32[16,126,128]{2,1,0:T(8,128)}, u32[]{:S(2)}) copy-start(f32[16,126,128]{2,1,0:T(8,128)} %get-tuple-element.355) | copy-start | bytes 3096580
  82.2 14.5 %copy-start.36 = (f32[16,124,128]{2,1,0:T(8,128)S(1)}, f32[16,124,128]{2,1,0:T(8,128)}, u32[]{:S(2)}) copy-start(f32[16,124,128]{2,1,0:T(8,128)} %get-tuple-element.358) | copy-start | bytes 3047428
  82.3 14.5 %copy-start.37 = (f32[16,124,128]{2,1,0:T(8,128)S(1)}, f32[16,124,128]{2,1,0:T(8,128)}, u32[]{:S(2)}) copy-start(f32[16,124,128]{2,1,0:T(8,128)} %get-tuple-element.359) | copy-start | bytes 3047428
  82.3 14.5 %copy-start.38 = (f32[16,127,128]{2,1,0:T(8,128)S(1)}, f32[16,127,128]{2,1,0:T(8,128)}, u32[]{:S(2)}) copy-start(f32[16,127,128]{2,1,0:T(8,128)} %get-tuple-element.352) | copy-start | bytes 3121156
  82.3 14.5 %copy-start.39 = (f32[16,127,128]{2,1,0:T(8,128)S(1)}, f32[16,127,128]{2,1,0:T(8,128)}, u32[]{:S(2)}) copy-start(f32[16,127,128]{2,1,0:T(8,128)} %get-tuple-element.353) | copy-start | bytes 3121156
  106.7 9.2 %collective-permute-start.7 = (f32[4,128,128]{2,1,0:T(8,128)S(1)}, f32[4,128,128]{2,1,0:T(8,128)S(1)}, u32[]{:S(2)}, u32[]{:S(2)}) collective-permute-start(f32[4,128,128]{2,1,0:T(8,128)S(1)} %bitcast.293), channel_id=1, source_target_pairs={{0,1},{1,2},{2,3},{3,4},{4,5},{5,6},{6,7},{7,8},{8,9},{9,10},{10,1... | collective-permute-start | bytes 786440 | tf_op jit(solution)/shard_map/ppermute | solution.py:21
  110.6 15.9 %copy-start.14 = (f32[16,128,128]{2,1,0:T(8,128)S(1)}, f32[16,128,128]{2,1,0:T(8,128)}, u32[]{:S(2)}) copy-start(f32[16,128,128]{2,1,0:T(8,128)} %param.25) | copy-start | bytes 3145732
  110.7 15.2 %collective-permute-start.6 = (f32[4,128,128]{2,1,0:T(8,128)S(1)}, f32[4,128,128]{2,1,0:T(8,128)S(1)}, u32[]{:S(2)}, u32[]{:S(2)}) collective-permute-start(f32[4,128,128]{2,1,0:T(8,128)S(1)} %bitcast.280), channel_id=1, source_target_pairs={{1,0},{2,1},{3,2},{4,3},{5,4},{6,5},{7,6},{8,7},{9,8},{10,9},{11,1... | collective-permute-start | bytes 786440 | tf_op jit(solution)/shard_map/ppermute | solution.py:23
  115.9 9.9 %copy-start.45 = (f32[4,128,128]{2,1,0:T(8,128)}, f32[4,128,128]{2,1,0:T(8,128)S(1)}, u32[]{:S(2)}) copy-start(f32[4,128,128]{2,1,0:T(8,128)S(1)} %collective-permute-done.7) | copy-start | bytes 786436
  138.6 8.3 %collective-permute-start.9 = (f32[4,128,128]{2,1,0:T(8,128)S(1)}, f32[4,128,128]{2,1,0:T(8,128)S(1)}, u32[]{:S(2)}, u32[]{:S(2)}) collective-permute-start(f32[4,128,128]{2,1,0:T(8,128)S(1)} %bitcast.294), channel_id=1, source_target_pairs={{0,1},{1,2},{2,3},{3,4},{4,5},{5,6},{6,7},{7,8},{8,9},{9,10},{10,1... | collective-permute-start | bytes 786440 | tf_op jit(solution)/shard_map/ppermute | solution.py:21
  141.5 15.8 %copy-start.7 = (f32[262144]{0:T(1024)S(1)}, f32[262144]{0:T(1024)}, u32[]{:S(2)}) copy-start(f32[262144]{0:T(1024)} %copy-done.6) | copy-start | bytes 3145732
  141.5 15.8 %copy-start.15 = (f32[16,128,128]{2,1,0:T(8,128)S(1)}, f32[16,128,128]{2,1,0:T(8,128)}, u32[]{:S(2)}) copy-start(f32[16,128,128]{2,1,0:T(8,128)} %param.25) | copy-start | bytes 3145732
  141.5 15.1 %collective-permute-start.8 = (f32[4,128,128]{2,1,0:T(8,128)S(1)}, f32[4,128,128]{2,1,0:T(8,128)S(1)}, u32[]{:S(2)}, u32[]{:S(2)}) collective-permute-start(f32[4,128,128]{2,1,0:T(8,128)S(1)} %bitcast.281), channel_id=1, source_target_pairs={{1,0},{2,1},{3,2},{4,3},{5,4},{6,5},{7,6},{8,7},{9,8},{10,9},{11,1... | collective-permute-start | bytes 786440 | tf_op jit(solution)/shard_map/ppermute | solution.py:23
  146.9 9.8 %copy-start.46 = (f32[4,128,128]{2,1,0:T(8,128)}, f32[4,128,128]{2,1,0:T(8,128)S(1)}, u32[]{:S(2)}) copy-start(f32[4,128,128]{2,1,0:T(8,128)S(1)} %collective-permute-done.9) | copy-start | bytes 786436
  167.3 8.0 %collective-permute-start.11 = (f32[4,128,128]{2,1,0:T(8,128)S(1)}, f32[4,128,128]{2,1,0:T(8,128)}, u32[]{:S(2)}, u32[]{:S(2)}) collective-permute-start(f32[4,128,128]{2,1,0:T(8,128)S(1)} %bitcast.295), channel_id=1, source_target_pairs={{0,1},{1,2},{2,3},{3,4},{4,5},{5,6},{6,7},{7,8},{8,9},{9,10},{10,1... | collective-permute-start | bytes 786440 | tf_op jit(solution)/shard_map/ppermute | solution.py:21
  170.3 15.6 %copy-start.16 = (f32[16,128,128]{2,1,0:T(8,128)S(1)}, f32[16,128,128]{2,1,0:T(8,128)}, u32[]{:S(2)}) copy-start(f32[16,128,128]{2,1,0:T(8,128)} %param.25) | copy-start | bytes 3145732
  170.3 15.6 %collective-permute-start.10 = (f32[4,128,128]{2,1,0:T(8,128)S(1)}, f32[4,128,128]{2,1,0:T(8,128)}, u32[]{:S(2)}, u32[]{:S(2)}) collective-permute-start(f32[4,128,128]{2,1,0:T(8,128)S(1)} %bitcast.282), channel_id=1, source_target_pairs={{1,0},{2,1},{3,2},{4,3},{5,4},{6,5},{7,6},{8,7},{9,8},{10,9},{11,1... | collective-permute-start | bytes 786440 | tf_op jit(solution)/shard_map/ppermute | solution.py:23
  218.8 7.0 collective-permute-start.13
  220.1 11.6 %copy-start.17 = (f32[16,128,128]{2,1,0:T(8,128)S(1)}, f32[16,128,128]{2,1,0:T(8,128)}, u32[]{:S(2)}) copy-start(f32[16,128,128]{2,1,0:T(8,128)} %param.25) | copy-start | bytes 3145732
  220.1 10.8 %collective-permute-start.12 = (f32[4,128,128]{2,1,0:T(8,128)S(1)}, f32[4,128,128]{2,1,0:T(8,128)S(1)}, u32[]{:S(2)}, u32[]{:S(2)}) collective-permute-start(f32[4,128,128]{2,1,0:T(8,128)S(1)} %bitcast.283), channel_id=1, source_target_pairs={{1,0},{2,1},{3,2},{4,3},{5,4},{6,5},{7,6},{8,7},{9,8},{10,9},{11,1... | collective-permute-start | bytes 786440 | tf_op jit(solution)/shard_map/ppermute | solution.py:23
  244.2 6.8 collective-permute-start.15
  246.2 11.4 %copy-start.18 = (f32[16,128,128]{2,1,0:T(8,128)S(1)}, f32[16,128,128]{2,1,0:T(8,128)}, u32[]{:S(2)}) copy-start(f32[16,128,128]{2,1,0:T(8,128)} %param.25) | copy-start | bytes 3145732
  246.2 10.6 %collective-permute-start.14 = (f32[4,128,128]{2,1,0:T(8,128)S(1)}, f32[4,128,128]{2,1,0:T(8,128)S(1)}, u32[]{:S(2)}, u32[]{:S(2)}) collective-permute-start(f32[4,128,128]{2,1,0:T(8,128)S(1)} %bitcast.284), channel_id=1, source_target_pairs={{1,0},{2,1},{3,2},{4,3},{5,4},{6,5},{7,6},{8,7},{9,8},{10,9},{11,1... | collective-permute-start | bytes 786440 | tf_op jit(solution)/shard_map/ppermute | solution.py:23
  267.5 6.9 collective-permute-start.17
  270.5 10.7 %copy-start.19 = (f32[16,128,128]{2,1,0:T(8,128)S(1)}, f32[16,128,128]{2,1,0:T(8,128)}, u32[]{:S(2)}) copy-start(f32[16,128,128]{2,1,0:T(8,128)} %param.25) | copy-start | bytes 3145732
  270.5 10.7 %collective-permute-start.16 = (f32[4,128,128]{2,1,0:T(8,128)S(1)}, f32[4,128,128]{2,1,0:T(8,128)}, u32[]{:S(2)}, u32[]{:S(2)}) collective-permute-start(f32[4,128,128]{2,1,0:T(8,128)S(1)} %bitcast.285), channel_id=1, source_target_pairs={{1,0},{2,1},{3,2},{4,3},{5,4},{6,5},{7,6},{8,7},{9,8},{10,9},{11,1... | collective-permute-start | bytes 786440 | tf_op jit(solution)/shard_map/ppermute | solution.py:23
  304.1 6.0 collective-permute-start.19
  305.7 9.8 %copy-start.12 = (f32[1,16,128,128]{3,2,1,0:T(8,128)S(1)}, f32[1,16,128,128]{3,2,1,0:T(8,128)}, u32[]{:S(2)}) copy-start(f32[1,16,128,128]{3,2,1,0:T(8,128)} %param.29) | copy-start | bytes 3145732
  305.7 9.7 %collective-permute-start.18 = (f32[4,128,128]{2,1,0:T(8,128)S(1)}, f32[4,128,128]{2,1,0:T(8,128)S(1)}, u32[]{:S(2)}, u32[]{:S(2)}) collective-permute-start(f32[4,128,128]{2,1,0:T(8,128)S(1)} %bitcast.286), channel_id=1, source_target_pairs={{1,0},{2,1},{3,2},{4,3},{5,4},{6,5},{7,6},{8,7},{9,8},{10,9},{11,1... | collective-permute-start | bytes 786440 | tf_op jit(solution)/shard_map/ppermute | solution.py:23
  323.7 6.5 collective-permute-start.21
  325.9 10.4 %copy-start.21 = (f32[16,128,128]{2,1,0:T(8,128)S(1)}, f32[16,128,128]{2,1,0:T(8,128)}, u32[]{:S(2)}) copy-start(f32[16,128,128]{2,1,0:T(8,128)} %param.25) | copy-start | bytes 3145732
  325.9 10.3 %collective-permute-start.20 = (f32[4,128,128]{2,1,0:T(8,128)S(1)}, f32[4,128,128]{2,1,0:T(8,128)S(1)}, u32[]{:S(2)}, u32[]{:S(2)}) collective-permute-start(f32[4,128,128]{2,1,0:T(8,128)S(1)} %bitcast.287), channel_id=1, source_target_pairs={{1,0},{2,1},{3,2},{4,3},{5,4},{6,5},{7,6},{8,7},{9,8},{10,9},{11,1... | collective-permute-start | bytes 786440 | tf_op jit(solution)/shard_map/ppermute | solution.py:23
  344.5 6.8 collective-permute-start.23
  346.8 10.8 %copy-start.22 = (f32[16,128,128]{2,1,0:T(8,128)S(1)}, f32[16,128,128]{2,1,0:T(8,128)}, u32[]{:S(2)}) copy-start(f32[16,128,128]{2,1,0:T(8,128)} %param.25) | copy-start | bytes 3145732
  346.8 10.7 %collective-permute-start.22 = (f32[4,128,128]{2,1,0:T(8,128)S(1)}, f32[4,128,128]{2,1,0:T(8,128)S(1)}, u32[]{:S(2)}, u32[]{:S(2)}) collective-permute-start(f32[4,128,128]{2,1,0:T(8,128)S(1)} %bitcast.288), channel_id=1, source_target_pairs={{1,0},{2,1},{3,2},{4,3},{5,4},{6,5},{7,6},{8,7},{9,8},{10,9},{11,1... | collective-permute-start | bytes 786440 | tf_op jit(solution)/shard_map/ppermute | solution.py:23
  369.7 6.9 collective-permute-start.25
  372.0 11.0 %copy-start.23 = (f32[16,128,128]{2,1,0:T(8,128)S(1)}, f32[16,128,128]{2,1,0:T(8,128)}, u32[]{:S(2)}) copy-start(f32[16,128,128]{2,1,0:T(8,128)} %param.25) | copy-start | bytes 3145732
  372.0 11.0 %collective-permute-start.24 = (f32[4,128,128]{2,1,0:T(8,128)S(1)}, f32[4,128,128]{2,1,0:T(8,128)S(1)}, u32[]{:S(2)}, u32[]{:S(2)}) collective-permute-start(f32[4,128,128]{2,1,0:T(8,128)S(1)} %bitcast.289), channel_id=1, source_target_pairs={{1,0},{2,1},{3,2},{4,3},{5,4},{6,5},{7,6},{8,7},{9,8},{10,9},{11,1... | collective-permute-start | bytes 786440 | tf_op jit(solution)/shard_map/ppermute | solution.py:23
  395.0 7.0 collective-permute-start.27
  397.3 11.1 %copy-start.1 = (f32[262144]{0:T(1024)S(1)}, f32[262144]{0:T(1024)}, u32[]{:S(2)}) copy-start(f32[262144]{0:T(1024)} %scatter_fusion.3) | copy-start | bytes 3145732
  397.3 11.1 %copy-start.24 = (f32[16,128,128]{2,1,0:T(8,128)S(1)}, f32[16,128,128]{2,1,0:T(8,128)}, u32[]{:S(2)}) copy-start(f32[16,128,128]{2,1,0:T(8,128)} %param.25) | copy-start | bytes 3145732
  397.3 11.1 %collective-permute-start.26 = (f32[4,128,128]{2,1,0:T(8,128)S(1)}, f32[4,128,128]{2,1,0:T(8,128)S(1)}, u32[]{:S(2)}, u32[]{:S(2)}) collective-permute-start(f32[4,128,128]{2,1,0:T(8,128)S(1)} %bitcast.290), channel_id=1, source_target_pairs={{1,0},{2,1},{3,2},{4,3},{5,4},{6,5},{7,6},{8,7},{9,8},{10,9},{11,1... | collective-permute-start | bytes 786440 | tf_op jit(solution)/shard_map/ppermute | solution.py:23
  421.6 7.0 collective-permute-start.29
  423.9 11.2 %copy-start.3 = (f32[262144]{0:T(1024)S(1)}, f32[262144]{0:T(1024)}, u32[]{:S(2)}) copy-start(f32[262144]{0:T(1024)} %scatter_fusion.4) | copy-start | bytes 3145732
  423.9 11.2 %copy-start.25 = (f32[16,128,128]{2,1,0:T(8,128)S(1)}, f32[16,128,128]{2,1,0:T(8,128)}, u32[]{:S(2)}) copy-start(f32[16,128,128]{2,1,0:T(8,128)} %param.25) | copy-start | bytes 3145732
  423.9 11.2 %collective-permute-start.28 = (f32[4,128,128]{2,1,0:T(8,128)S(1)}, f32[4,128,128]{2,1,0:T(8,128)S(1)}, u32[]{:S(2)}, u32[]{:S(2)}) collective-permute-start(f32[4,128,128]{2,1,0:T(8,128)S(1)} %bitcast.291), channel_id=1, source_target_pairs={{1,0},{2,1},{3,2},{4,3},{5,4},{6,5},{7,6},{8,7},{9,8},{10,9},{11,1... | collective-permute-start | bytes 786440 | tf_op jit(solution)/shard_map/ppermute | solution.py:23
  448.3 7.0 collective-permute-start.31
  450.6 11.2 %copy-start.5 = (f32[262144]{0:T(1024)S(1)}, f32[262144]{0:T(1024)}, u32[]{:S(2)}) copy-start(f32[262144]{0:T(1024)} %scatter_fusion.5) | copy-start | bytes 3145732
  450.6 11.1 %copy-start.26 = (f32[16,128,128]{2,1,0:T(8,128)S(1)}, f32[16,128,128]{2,1,0:T(8,128)}, u32[]{:S(2)}) copy-start(f32[16,128,128]{2,1,0:T(8,128)} %param.25) | copy-start | bytes 3145732
  450.6 11.1 %collective-permute-start.30 = (f32[4,128,128]{2,1,0:T(8,128)S(1)}, f32[4,128,128]{2,1,0:T(8,128)S(1)}, u32[]{:S(2)}, u32[]{:S(2)}) collective-permute-start(f32[4,128,128]{2,1,0:T(8,128)S(1)} %bitcast.292), channel_id=1, source_target_pairs={{1,0},{2,1},{3,2},{4,3},{5,4},{6,5},{7,6},{8,7},{9,8},{10,9},{11,1... | collective-permute-start | bytes 786440 | tf_op jit(solution)/shard_map/ppermute | solution.py:23
  658.2 39.9 %copy-start.27 = (f32[16,128,128]{2,1,0:T(8,128)S(1)}, f32[16,128,128]{2,1,0:T(8,128)}, u32[]{:S(2)}) copy-start(f32[16,128,128]{2,1,0:T(8,128)} %param.25) | copy-start | bytes 3145732
  (25 other events, 95.8 us)
Sparse Core Ops, SparseCore 0:
  479.6 171.1 all-gather.2
